TPU v7x, 32 devices: a whole 2x2x4 slice. The times are simulated.
32 devices in a mesh: grp: 2 (over y), cell: 4 (over z), snap: 2 (over x), var: 2 (over core).
Axes of the slice: x: 2, y: 2, z: 4, core: 2. Of those that a mesh axis runs over, the one named last changes fastest.
Arguments:
- q_true: bfloat16 [64, 10, 2048], P(('snap', 'var'), 'grp', 'cell'), parts along dimension 1, may hold values from -6 to 6
- coeffs: bfloat16 [64, 256], P(('snap', 'var'), 'grp'), parts along dimension 1, may hold values from -0.5 to 0.5
- basis: bfloat16 [128, 10, 2048], P(('snap', 'var'), 'grp', 'cell'), parts along dimension 1, may hold values from -6 to 6
- weights: float32 [10, 2048], P('grp', 'cell'), parts along dimension 0, may hold values from 0.0029646354 to 0.029646354
- geometry: float32 [12, 2048], P('grp', 'cell'), parts along dimension 0, may hold values from 0.2 to 1
- neighbors: int32 [12, 2048], P('grp', 'cell'), parts along dimension 0, may hold values from 0 to 767, as said below
- send_rows: int32 [4, 4, 128], P('cell', 'grp'), parts along dimension 1, may hold values from 0 to 511, as said below
- block_count: int32 [4, 2], P('cell', 'grp'), parts along dimension 1, may hold values from 2 to 4
Outputs:
- closure: float32 [64, 256], P(('snap', 'var'), 'grp'), parts along dimension 1
There are 2 independent parts, one for each index of `grp`. A program takes and returns all parts, laid end to end along the dimension named above; each array names one. Nothing has to cross between parts.
Inputs may be any that keep to these rules, and one draw needn't show every extreme that they name: neighbors[k, c] indexes a list made of the 512 cells of c's own cell shard, then the 128 cells received from the shard before, then the 128 cells received from the shard after. `send_rows`: indices local to the sending cell shard.
All inputs are finite; a program needn't handle non-finite values.
Results may differ from a plain program's by a relative error of at most 0.00091.
Values may be sent and summed in bfloat16 or wider, within the bound.
A program may use at most 64 MiB of HBM per device.

v0:
```python
import math
import jax
import jax.numpy as jnp
from jax import lax
from jax.sharding import PartitionSpec as P

BLOCK = 128


def from_behind(shard, axis, by):
    peers = lax.axis_size(axis)
    pairs = [(i, i + by) for i in range(peers) if 0 <= i + by < peers]
    return lax.ppermute(shard, axis, pairs)


def face_flux(extended, geometry, neighbors):
    cell_count = geometry.shape[1]
    var_count = extended.shape[1]
    own_cells = extended[:, :, :cell_count]
    product = extended * extended[:, 1:2, :]
    own_product = product[:, :, :cell_count]
    stacked = jnp.concatenate([extended, product], axis=1)
    running = jnp.zeros(own_cells.shape, jnp.float32)
    for face_index in range(geometry.shape[0]):
        taken = jnp.take(stacked, neighbors[face_index], axis=2)
        beside = taken[:, :var_count]
        beside_product = taken[:, var_count:]
        running = running + geometry[face_index] * (
            0.5 * (own_product + beside_product) - 0.5 * (beside - own_cells)
        )
    return running


def local(q_true, coeffs, basis, weights, geometry, neighbors, send_rows, block_count):
    snap_count, var_count, cell_count = q_true.shape
    send_lists = send_rows[0]

    def rim_rows(field):
        return (jnp.take(field, send_lists[0], axis=2), jnp.take(field, send_lists[1], axis=2))

    true_to_prev, true_to_next = rim_rows(q_true)
    whole_basis = lax.all_gather(basis, ("snap", "var"), axis=0, tiled=True)
    basis_flat = whole_basis.reshape(whole_basis.shape[0], var_count * cell_count)
    rebuilt_sum = jnp.dot(coeffs, basis_flat, preferred_element_type=jnp.float32)
    rebuilt = rebuilt_sum.astype(jnp.bfloat16).reshape(snap_count, var_count, cell_count)
    rebuilt_to_prev, rebuilt_to_next = rim_rows(rebuilt)
    true_from_prev = from_behind(true_to_next, "cell", 1)
    true_from_next = from_behind(true_to_prev, "cell", -1)
    rebuilt_from_prev = from_behind(rebuilt_to_next, "cell", 1)
    rebuilt_from_next = from_behind(rebuilt_to_prev, "cell", -1)
    true_ext = jnp.concatenate([q_true, true_from_prev, true_from_next], axis=2)
    rebuilt_ext = jnp.concatenate([rebuilt, rebuilt_from_prev, rebuilt_from_next], axis=2)
    positions = jnp.arange(cell_count, dtype=jnp.int32)
    live = (positions < block_count[0, 0] * BLOCK).astype(jnp.float32)
    group = math.gcd(snap_count, 8)
    ext_count = true_ext.shape[2]

    def snap_block(pair):
        true_part, rebuilt_part = pair
        flux_true = face_flux(true_part.astype(jnp.float32), geometry, neighbors)
        flux_rebuilt = face_flux(rebuilt_part.astype(jnp.float32), geometry, neighbors)
        return (weights * live * (flux_true - flux_rebuilt)).astype(jnp.bfloat16)

    true_groups = true_ext.reshape(snap_count // group, group, var_count, ext_count)
    rebuilt_groups = rebuilt_ext.reshape(snap_count // group, group, var_count, ext_count)
    weighted = lax.map(snap_block, (true_groups, rebuilt_groups))
    weighted_flat = weighted.reshape(snap_count, var_count * cell_count)
    contract = (((1,), (1,)), ((), ()))
    closure_part = lax.dot_general(
        weighted_flat, basis_flat, contract, preferred_element_type=jnp.float32
    )
    return lax.psum(closure_part, "cell")


def solution(mesh):
    in_specs = (
        P(("snap", "var"), "grp", "cell"),
        P(("snap", "var"), "grp"),
        P(("snap", "var"), "grp", "cell"),
        P("grp", "cell"),
        P("grp", "cell"),
        P("grp", "cell"),
        P("cell", "grp", None),
        P("cell", "grp"),
    )
    out_specs = P(("snap", "var"), "grp")
    return jax.shard_map(local, mesh=mesh, in_specs=in_specs, out_specs=out_specs, check_vma=False)
```

profile of v0, /device:TPU:0, one launch (start us, length us, event | category | flops | bytes accessed | tf_op | source)
XLA Modules:
  0.0 230.5 jit_solution(12883758674813576312)
XLA Ops:
  0.8 9.7 %all_gather.3 = bf16[128,5,512]{2,0,1:T(8,128)(2,1)S(1)} all-gather(bf16[32,5,512]{2,0,1:T(8,128)(2,1)} %param.16), channel_id=1, replica_groups=mesh['grp'=2,'cell'=4,'snap'=2,'var'=2] {'snap','var'}, dimensions={0}, use_global_device_ids=true | all-gather | bytes 819200 | tf_op jit(solution)/shard_map/all_gather | solution.py:42
  15.2 3.5 %collective-permute-start = (bf16[16,5,128]{0,1,2:T(8,128)(2,1)}, bf16[16,5,128]{0,1,2:T(8,128)(2,1)S(1)}, u32[]{:S(2)}, u32[]{:S(2)}) collective-permute-start(bf16[16,5,128]{0,1,2:T(8,128)(2,1)} %get-tuple-element.158), channel_id=1, source_target_pairs={{0,4},{4,8},{8,12},{1,5},{5,9},{9,13},{2,6},{6,10},{10,14},{3,7},{... | collective-permute-start | bytes 61448 | tf_op jit(solution)/shard_map/ppermute | solution.py:13
  21.6 4.6 %collective-permute-start.2 = (bf16[16,5,128]{0,1,2:T(8,128)(2,1)}, bf16[16,5,128]{0,1,2:T(8,128)(2,1)S(1)}, u32[]{:S(2)}, u32[]{:S(2)}) collective-permute-start(bf16[16,5,128]{0,1,2:T(8,128)(2,1)} %get-tuple-element.157), channel_id=1, source_target_pairs={{0,4},{4,8},{8,12},{1,5},{5,9},{9,13},{2,6},{6,10},{10,14},{3,7},{... | collective-permute-start | bytes 61448 | tf_op jit(solution)/shard_map/ppermute | solution.py:13
  32.1 4.0 %collective-permute-done.3 = bf16[16,5,128]{0,1,2:T(8,128)(2,1)S(1)} collective-permute-done((bf16[16,5,128]{0,1,2:T(8,128)(2,1)S(1)}, bf16[16,5,128]{0,1,2:T(8,128)(2,1)S(1)}, u32[]{:S(2)}, u32[]{:S(2)}) %collective-permute-start.3) | collective-permute-done | bytes 20512 | tf_op jit(solution)/shard_map/ppermute | solution.py:13
  36.9 181.6 %while.11 = (s32[]{:T(128)}, bf16[2,8,5,512]{3,1,2,0:T(8,128)(2,1)}, f32[5,512]{1,0:T(8,128)S(1)}, f32[6,512]{1,0:T(8,128)}, bf16[2,8,5,768]{3,1,0,2:T(8,128)(2,...) while((s32[]{:T(128)}, ...), condition=%wide.region_1.4_spmd.clone, body=%wide.region_0.3_spmd.clone.sunk | while | flops 2576898 | bytes 26133308 | solution.py:66
  49.7 2.8 %gather_fusion.11 = f32[512,8,10]{2,1,0:T(8,128)} fusion(f32[8,10,768]{1,0,2:T(8,128)S(1)} %copy.153, s32[1024]{0:T(1024)} %pad_clamp_fusion.19), kind=kCustom, calls=%fused_computation.10.clone.clone.1 | custom fusion | bytes 329728 | tf_op jit(solution)/shard_map/while/body/eval_jaxpr/jit(_take)/gather | solution.py:25
  52.5 2.9 %copy.164 = f32[512,8,10]{0,1,2:T(8,128)} copy(f32[512,8,10]{2,1,0:T(8,128)} %gather_fusion.11) | data formatting | bytes 327680 | tf_op jit(solution)/shard_map/while/body/eval_jaxpr/jit(_take)/gather | solution.py:25
  55.4 2.7 %gather_fusion.9 = f32[512,8,10]{2,1,0:T(8,128)} fusion(f32[8,10,768]{1,0,2:T(8,128)S(1)} %copy.153, s32[1024]{0:T(1024)S(1)} %pad_clamp_fusion.18), kind=kCustom, calls=%fused_computation.11.clone.clone.1 | custom fusion | bytes 329728 | tf_op jit(solution)/shard_map/while/body/eval_jaxpr/jit(_take)/gather | solution.py:25
  58.1 2.9 %copy.162 = f32[512,8,10]{0,1,2:T(8,128)} copy(f32[512,8,10]{2,1,0:T(8,128)} %gather_fusion.9) | data formatting | bytes 327680 | tf_op jit(solution)/shard_map/while/body/eval_jaxpr/jit(_take)/gather | solution.py:25
  61.0 2.7 %gather_fusion.7 = f32[512,8,10]{2,1,0:T(8,128)} fusion(f32[8,10,768]{1,0,2:T(8,128)S(1)} %copy.153, s32[1024]{0:T(1024)S(1)} %pad_clamp_fusion.17), kind=kCustom, calls=%fused_computation.12.clone.clone.1 | custom fusion | bytes 329728 | tf_op jit(solution)/shard_map/while/body/eval_jaxpr/jit(_take)/gather | solution.py:25
  63.6 2.9 %copy.160 = f32[512,8,10]{0,1,2:T(8,128)} copy(f32[512,8,10]{2,1,0:T(8,128)} %gather_fusion.7) | data formatting | bytes 327680 | tf_op jit(solution)/shard_map/while/body/eval_jaxpr/jit(_take)/gather | solution.py:25
  66.5 2.7 %gather_fusion.5 = f32[512,8,10]{2,1,0:T(8,128)} fusion(f32[8,10,768]{1,0,2:T(8,128)S(1)} %copy.153, s32[1024]{0:T(1024)S(1)} %pad_clamp_fusion.16), kind=kCustom, calls=%fused_computation.13.clone.clone.1 | custom fusion | bytes 329728 | tf_op jit(solution)/shard_map/while/body/eval_jaxpr/jit(_take)/gather | solution.py:25
  69.2 2.9 %copy.158 = f32[512,8,10]{0,1,2:T(8,128)} copy(f32[512,8,10]{2,1,0:T(8,128)} %gather_fusion.5) | data formatting | bytes 327680 | tf_op jit(solution)/shard_map/while/body/eval_jaxpr/jit(_take)/gather | solution.py:25
  72.1 2.7 %gather_fusion.3 = f32[512,8,10]{2,1,0:T(8,128)} fusion(f32[8,10,768]{1,0,2:T(8,128)S(1)} %copy.153, s32[1024]{0:T(1024)S(1)} %pad_clamp_fusion.15), kind=kCustom, calls=%fused_computation.14.clone.clone.1 | custom fusion | bytes 329728 | tf_op jit(solution)/shard_map/while/body/eval_jaxpr/jit(_take)/gather | solution.py:25
  74.8 2.9 %copy.156 = f32[512,8,10]{0,1,2:T(8,128)} copy(f32[512,8,10]{2,1,0:T(8,128)} %gather_fusion.3) | data formatting | bytes 327680 | tf_op jit(solution)/shard_map/while/body/eval_jaxpr/jit(_take)/gather | solution.py:25
  77.7 2.7 %gather_fusion.1 = f32[512,8,10]{2,1,0:T(8,128)} fusion(f32[8,10,768]{1,0,2:T(8,128)S(1)} %copy.153, s32[1024]{0:T(1024)S(1)} %pad_clamp_fusion.14), kind=kCustom, calls=%fused_computation.15.clone.clone.1 | custom fusion | bytes 329728 | tf_op jit(solution)/shard_map/while/body/eval_jaxpr/jit(_take)/gather | solution.py:25
  80.3 2.9 %copy.154 = f32[512,8,10]{0,1,2:T(8,128)} copy(f32[512,8,10]{2,1,0:T(8,128)} %gather_fusion.1) | data formatting | bytes 327680 | tf_op jit(solution)/shard_map/while/body/eval_jaxpr/jit(_take)/gather | solution.py:25
  85.4 2.8 %gather_fusion.10 = f32[512,8,10]{2,1,0:T(8,128)} fusion(f32[8,10,768]{1,0,2:T(8,128)S(1)} %copy.151, s32[1024]{0:T(1024)} %pad_clamp_fusion.19), kind=kCustom, calls=%fused_computation.1.clone.clone.1 | custom fusion | bytes 329728 | tf_op jit(solution)/shard_map/while/body/eval_jaxpr/jit(_take)/gather | solution.py:25
  88.2 2.9 %copy.163 = f32[512,8,10]{0,1,2:T(8,128)} copy(f32[512,8,10]{2,1,0:T(8,128)} %gather_fusion.10) | data formatting | bytes 327680 | tf_op jit(solution)/shard_map/while/body/eval_jaxpr/jit(_take)/gather | solution.py:25
  95.5 2.9 %copy.161 = f32[512,8,10]{0,1,2:T(8,128)} copy(f32[512,8,10]{2,1,0:T(8,128)} %gather_fusion.8) | data formatting | bytes 327680 | tf_op jit(solution)/shard_map/while/body/eval_jaxpr/jit(_take)/gather | solution.py:25
  100.2 2.7 %gather_fusion.6 = f32[512,8,10]{2,1,0:T(8,128)} fusion(f32[8,10,768]{1,0,2:T(8,128)S(1)} %copy.151, s32[1024]{0:T(1024)S(1)} %pad_clamp_fusion.17), kind=kCustom, calls=%fused_computation.6.clone.clone.1 | custom fusion | bytes 329728 | tf_op jit(solution)/shard_map/while/body/eval_jaxpr/jit(_take)/gather | solution.py:25
  102.9 2.9 %copy.159 = f32[512,8,10]{0,1,2:T(8,128)} copy(f32[512,8,10]{2,1,0:T(8,128)} %gather_fusion.6) | data formatting | bytes 327680 | tf_op jit(solution)/shard_map/while/body/eval_jaxpr/jit(_take)/gather | solution.py:25
  107.6 2.7 %gather_fusion.4 = f32[512,8,10]{2,1,0:T(8,128)} fusion(f32[8,10,768]{1,0,2:T(8,128)S(1)} %copy.151, s32[1024]{0:T(1024)S(1)} %pad_clamp_fusion.16), kind=kCustom, calls=%fused_computation.7.clone.clone.1 | custom fusion | bytes 329728 | tf_op jit(solution)/shard_map/while/body/eval_jaxpr/jit(_take)/gather | solution.py:25
  110.3 2.9 %copy.157 = f32[512,8,10]{0,1,2:T(8,128)} copy(f32[512,8,10]{2,1,0:T(8,128)} %gather_fusion.4) | data formatting | bytes 327680 | tf_op jit(solution)/shard_map/while/body/eval_jaxpr/jit(_take)/gather | solution.py:25
  114.9 2.7 %gather_fusion.2 = f32[512,8,10]{2,1,0:T(8,128)} fusion(f32[8,10,768]{1,0,2:T(8,128)S(1)} %copy.151, s32[1024]{0:T(1024)S(1)} %pad_clamp_fusion.15), kind=kCustom, calls=%fused_computation.8.clone.clone.1 | custom fusion | bytes 329728 | tf_op jit(solution)/shard_map/while/body/eval_jaxpr/jit(_take)/gather | solution.py:25
  117.6 2.9 %copy.155 = f32[512,8,10]{0,1,2:T(8,128)} copy(f32[512,8,10]{2,1,0:T(8,128)} %gather_fusion.2) | data formatting | bytes 327680 | tf_op jit(solution)/shard_map/while/body/eval_jaxpr/jit(_take)/gather | solution.py:25
  120.5 2.7 %gather_fusion = f32[512,8,10]{2,1,0:T(8,128)} fusion(f32[8,10,768]{1,0,2:T(8,128)S(1)} %copy.151, s32[1024]{0:T(1024)S(1)} %pad_clamp_fusion.14), kind=kCustom, calls=%fused_computation.9.clone.clone.1 | custom fusion | bytes 329728 | tf_op jit(solution)/shard_map/while/body/eval_jaxpr/jit(_take)/gather | solution.py:25
  140.5 2.8 %gather_fusion.11 = f32[512,8,10]{2,1,0:T(8,128)} fusion(f32[8,10,768]{1,0,2:T(8,128)S(1)} %copy.153, s32[1024]{0:T(1024)} %pad_clamp_fusion.19), kind=kCustom, calls=%fused_computation.10.clone.clone.1 | custom fusion | bytes 329728 | tf_op jit(solution)/shard_map/while/body/eval_jaxpr/jit(_take)/gather | solution.py:25
  143.3 2.9 %copy.164 = f32[512,8,10]{0,1,2:T(8,128)} copy(f32[512,8,10]{2,1,0:T(8,128)} %gather_fusion.11) | data formatting | bytes 327680 | tf_op jit(solution)/shard_map/while/body/eval_jaxpr/jit(_take)/gather | solution.py:25
  146.2 2.7 %gather_fusion.9 = f32[512,8,10]{2,1,0:T(8,128)} fusion(f32[8,10,768]{1,0,2:T(8,128)S(1)} %copy.153, s32[1024]{0:T(1024)S(1)} %pad_clamp_fusion.18), kind=kCustom, calls=%fused_computation.11.clone.clone.1 | custom fusion | bytes 329728 | tf_op jit(solution)/shard_map/while/body/eval_jaxpr/jit(_take)/gather | solution.py:25
  148.9 2.9 %copy.162 = f32[512,8,10]{0,1,2:T(8,128)} copy(f32[512,8,10]{2,1,0:T(8,128)} %gather_fusion.9) | data formatting | bytes 327680 | tf_op jit(solution)/shard_map/while/body/eval_jaxpr/jit(_take)/gather | solution.py:25
  151.7 2.7 %gather_fusion.7 = f32[512,8,10]{2,1,0:T(8,128)} fusion(f32[8,10,768]{1,0,2:T(8,128)S(1)} %copy.153, s32[1024]{0:T(1024)S(1)} %pad_clamp_fusion.17), kind=kCustom, calls=%fused_computation.12.clone.clone.1 | custom fusion | bytes 329728 | tf_op jit(solution)/shard_map/while/body/eval_jaxpr/jit(_take)/gather | solution.py:25
  154.4 2.9 %copy.160 = f32[512,8,10]{0,1,2:T(8,128)} copy(f32[512,8,10]{2,1,0:T(8,128)} %gather_fusion.7) | data formatting | bytes 327680 | tf_op jit(solution)/shard_map/while/body/eval_jaxpr/jit(_take)/gather | solution.py:25
  157.3 2.7 %gather_fusion.5 = f32[512,8,10]{2,1,0:T(8,128)} fusion(f32[8,10,768]{1,0,2:T(8,128)S(1)} %copy.153, s32[1024]{0:T(1024)S(1)} %pad_clamp_fusion.16), kind=kCustom, calls=%fused_computation.13.clone.clone.1 | custom fusion | bytes 329728 | tf_op jit(solution)/shard_map/while/body/eval_jaxpr/jit(_take)/gather | solution.py:25
  160.0 2.9 %copy.158 = f32[512,8,10]{0,1,2:T(8,128)} copy(f32[512,8,10]{2,1,0:T(8,128)} %gather_fusion.5) | data formatting | bytes 327680 | tf_op jit(solution)/shard_map/while/body/eval_jaxpr/jit(_take)/gather | solution.py:25
  165.6 2.9 %copy.156 = f32[512,8,10]{0,1,2:T(8,128)} copy(f32[512,8,10]{2,1,0:T(8,128)} %gather_fusion.3) | data formatting | bytes 327680 | tf_op jit(solution)/shard_map/while/body/eval_jaxpr/jit(_take)/gather | solution.py:25
  171.1 2.9 %copy.154 = f32[512,8,10]{0,1,2:T(8,128)} copy(f32[512,8,10]{2,1,0:T(8,128)} %gather_fusion.1) | data formatting | bytes 327680 | tf_op jit(solution)/shard_map/while/body/eval_jaxpr/jit(_take)/gather | solution.py:25
  176.2 2.8 %gather_fusion.10 = f32[512,8,10]{2,1,0:T(8,128)} fusion(f32[8,10,768]{1,0,2:T(8,128)S(1)} %copy.151, s32[1024]{0:T(1024)} %pad_clamp_fusion.19), kind=kCustom, calls=%fused_computation.1.clone.clone.1 | custom fusion | bytes 329728 | tf_op jit(solution)/shard_map/while/body/eval_jaxpr/jit(_take)/gather | solution.py:25
  179.0 2.9 %copy.163 = f32[512,8,10]{0,1,2:T(8,128)} copy(f32[512,8,10]{2,1,0:T(8,128)} %gather_fusion.10) | data formatting | bytes 327680 | tf_op jit(solution)/shard_map/while/body/eval_jaxpr/jit(_take)/gather | solution.py:25
  186.3 2.9 %copy.161 = f32[512,8,10]{0,1,2:T(8,128)} copy(f32[512,8,10]{2,1,0:T(8,128)} %gather_fusion.8) | data formatting | bytes 327680 | tf_op jit(solution)/shard_map/while/body/eval_jaxpr/jit(_take)/gather | solution.py:25
  191.0 2.7 %gather_fusion.6 = f32[512,8,10]{2,1,0:T(8,128)} fusion(f32[8,10,768]{1,0,2:T(8,128)S(1)} %copy.151, s32[1024]{0:T(1024)S(1)} %pad_clamp_fusion.17), kind=kCustom, calls=%fused_computation.6.clone.clone.1 | custom fusion | bytes 329728 | tf_op jit(solution)/shard_map/while/body/eval_jaxpr/jit(_take)/gather | solution.py:25
  193.7 2.9 %copy.159 = f32[512,8,10]{0,1,2:T(8,128)} copy(f32[512,8,10]{2,1,0:T(8,128)} %gather_fusion.6) | data formatting | bytes 327680 | tf_op jit(solution)/shard_map/while/body/eval_jaxpr/jit(_take)/gather | solution.py:25
  198.3 2.7 %gather_fusion.4 = f32[512,8,10]{2,1,0:T(8,128)} fusion(f32[8,10,768]{1,0,2:T(8,128)S(1)} %copy.151, s32[1024]{0:T(1024)S(1)} %pad_clamp_fusion.16), kind=kCustom, calls=%fused_computation.7.clone.clone.1 | custom fusion | bytes 329728 | tf_op jit(solution)/shard_map/while/body/eval_jaxpr/jit(_take)/gather | solution.py:25
  201.1 2.9 %copy.157 = f32[512,8,10]{0,1,2:T(8,128)} copy(f32[512,8,10]{2,1,0:T(8,128)} %gather_fusion.4) | data formatting | bytes 327680 | tf_op jit(solution)/shard_map/while/body/eval_jaxpr/jit(_take)/gather | solution.py:25
  205.7 2.7 %gather_fusion.2 = f32[512,8,10]{2,1,0:T(8,128)} fusion(f32[8,10,768]{1,0,2:T(8,128)S(1)} %copy.151, s32[1024]{0:T(1024)S(1)} %pad_clamp_fusion.15), kind=kCustom, calls=%fused_computation.8.clone.clone.1 | custom fusion | bytes 329728 | tf_op jit(solution)/shard_map/while/body/eval_jaxpr/jit(_take)/gather | solution.py:25
  208.4 2.9 %copy.155 = f32[512,8,10]{0,1,2:T(8,128)} copy(f32[512,8,10]{2,1,0:T(8,128)} %gather_fusion.2) | data formatting | bytes 327680 | tf_op jit(solution)/shard_map/while/body/eval_jaxpr/jit(_take)/gather | solution.py:25
  211.3 2.7 %gather_fusion = f32[512,8,10]{2,1,0:T(8,128)} fusion(f32[8,10,768]{1,0,2:T(8,128)S(1)} %copy.151, s32[1024]{0:T(1024)S(1)} %pad_clamp_fusion.14), kind=kCustom, calls=%fused_computation.9.clone.clone.1 | custom fusion | bytes 329728 | tf_op jit(solution)/shard_map/while/body/eval_jaxpr/jit(_take)/gather | solution.py:25
  219.8 10.7 %psum.7 = f32[16,128]{1,0:T(8,128)} all-reduce(f32[16,128]{1,0:T(8,128)S(1)} %fusion.66), channel_id=1, replica_groups=mesh['grp'=2,'cell'=4,'snap'=2,'var'=2] {'cell'}, use_global_device_ids=true, to_apply=%region_2.5 | all-reduce | flops 2048 | bytes 16384 | tf_op jit(solution)/shard_map/psum | solution.py:72
  (217 shorter events, 78.7 us)
Async XLA Ops:
  0.0 10.8 %copy-start = (bf16[16,128]{1,0:T(8,128)(2,1)S(1)}, bf16[16,128]{1,0:T(8,128)(2,1)}, u32[]{:S(2)}) copy-start(bf16[16,128]{1,0:T(8,128)(2,1)} %param.15) | copy-start | bytes 12292
  0.8 11.3 %copy-start.17 = (bf16[16,5,512]{2,0,1:T(8,128)(2,1)S(1)}, bf16[16,5,512]{2,0,1:T(8,128)(2,1)}, u32[]{:S(2)}) copy-start(bf16[16,5,512]{2,0,1:T(8,128)(2,1)} %param.14) | copy-start | bytes 245764
  10.8 4.4 %copy-start.14 = (bf16[128,5,512]{0,2,1:T(8,128)(2,1)}, bf16[128,5,512]{0,2,1:T(8,128)(2,1)S(1)}, u32[]{:S(2)}) copy-start(bf16[128,5,512]{0,2,1:T(8,128)(2,1)S(1)} %copy.124) | copy-start | bytes 1966084
  12.8 24.1 %copy-start.15 = (f32[5,512]{1,0:T(8,128)S(1)}, f32[5,512]{1,0:T(8,128)}, u32[]{:S(2)}) copy-start(f32[5,512]{1,0:T(8,128)} %param.17) | copy-start | bytes 30724
  15.2 12.9 %collective-permute-start = (bf16[16,5,128]{0,1,2:T(8,128)(2,1)}, bf16[16,5,128]{0,1,2:T(8,128)(2,1)S(1)}, u32[]{:S(2)}, u32[]{:S(2)}) collective-permute-start(bf16[16,5,128]{0,1,2:T(8,128)(2,1)} %get-tuple-element.158), channel_id=1, source_target_pairs={{0,4},{4,8},{8,12},{1,5},{5,9},{9,13},{2,6},{6,10},{10,14},{3,7},{... | collective-permute-start | bytes 61448 | tf_op jit(solution)/shard_map/ppermute | solution.py:13
  20.3 10.4 %collective-permute-start.1 = (bf16[16,5,128]{0,1,2:T(8,128)(2,1)S(1)}, bf16[16,5,128]{0,1,2:T(8,128)(2,1)S(1)}, u32[]{:S(2)}, u32[]{:S(2)}) collective-permute-start(bf16[16,5,128]{0,1,2:T(8,128)(2,1)S(1)} %get-tuple-element.160), channel_id=1, source_target_pairs={{4,0},{8,4},{12,8},{5,1},{9,5},{13,9},{6,2},{10,6},{14,10},{7,3},{... | collective-permute-start | bytes 61448 | tf_op jit(solution)/shard_map/ppermute | solution.py:13
  21.6 10.4 %collective-permute-start.2 = (bf16[16,5,128]{0,1,2:T(8,128)(2,1)}, bf16[16,5,128]{0,1,2:T(8,128)(2,1)S(1)}, u32[]{:S(2)}, u32[]{:S(2)}) collective-permute-start(bf16[16,5,128]{0,1,2:T(8,128)(2,1)} %get-tuple-element.157), channel_id=1, source_target_pairs={{0,4},{4,8},{8,12},{1,5},{5,9},{9,13},{2,6},{6,10},{10,14},{3,7},{... | collective-permute-start | bytes 61448 | tf_op jit(solution)/shard_map/ppermute | solution.py:13
  26.2 9.9 %collective-permute-start.3 = (bf16[16,5,128]{0,1,2:T(8,128)(2,1)S(1)}, bf16[16,5,128]{0,1,2:T(8,128)(2,1)S(1)}, u32[]{:S(2)}, u32[]{:S(2)}) collective-permute-start(bf16[16,5,128]{0,1,2:T(8,128)(2,1)S(1)} %get-tuple-element.159), channel_id=1, source_target_pairs={{4,0},{8,4},{12,8},{5,1},{9,5},{13,9},{6,2},{10,6},{14,10},{7,3},{... | collective-permute-start | bytes 61448 | tf_op jit(solution)/shard_map/ppermute | solution.py:13
  98.4 7.4 %copy-start.28 = (pred[512]{0:T(512)(128)(4,1)S(1)}, pred[512]{0:T(512)(128)(4,1)}, u32[]{:S(2)}) copy-start(pred[512]{0:T(512)(128)(4,1)} %compare_and_fusion.17) | copy-start | bytes 1540 | tf_op jit(solution)/shard_map/while
  105.8 7.4 %copy-start.27 = (pred[512]{0:T(512)(128)(4,1)S(1)}, pred[512]{0:T(512)(128)(4,1)}, u32[]{:S(2)}) copy-start(pred[512]{0:T(512)(128)(4,1)} %compare_and_fusion.16) | copy-start | bytes 1540 | tf_op jit(solution)/shard_map/while
  120.5 6.1 %copy-start.18 = (f32[1,512]{1,0:T(1,128)S(1)}, f32[1,512]{1,0:T(1,128)}, u32[]{:S(2)}) copy-start(f32[1,512]{1,0:T(1,128)} %get-tuple-element.261) | copy-start | bytes 6148 | tf_op jit(solution)/shard_map/while
  120.5 6.1 %copy-start.19 = (f32[1,512]{1,0:T(1,128)S(1)}, f32[1,512]{1,0:T(1,128)}, u32[]{:S(2)}) copy-start(f32[1,512]{1,0:T(1,128)} %get-tuple-element.251) | copy-start | bytes 6148 | tf_op jit(solution)/shard_map/while
  120.5 6.1 %copy-start.20 = (f32[1,512]{1,0:T(1,128)S(1)}, f32[1,512]{1,0:T(1,128)}, u32[]{:S(2)}) copy-start(f32[1,512]{1,0:T(1,128)} %get-tuple-element.253) | copy-start | bytes 6148 | tf_op jit(solution)/shard_map/while
  120.5 6.1 %copy-start.21 = (f32[1,512]{1,0:T(1,128)S(1)}, f32[1,512]{1,0:T(1,128)}, u32[]{:S(2)}) copy-start(f32[1,512]{1,0:T(1,128)} %get-tuple-element.255) | copy-start | bytes 6148 | tf_op jit(solution)/shard_map/while
  123.2 3.3 %copy-start.5 = (f32[512,8,10]{0,1,2:T(8,128)S(1)}, f32[512,8,10]{0,1,2:T(8,128)}, u32[]{:S(2)}) copy-start(f32[512,8,10]{0,1,2:T(8,128)} %copy.155) | copy-start | bytes 491524 | tf_op jit(solution)/shard_map/while
  123.2 3.3 %copy-start.26 = (pred[512]{0:T(512)(128)(4,1)S(1)}, pred[512]{0:T(512)(128)(4,1)}, u32[]{:S(2)}) copy-start(pred[512]{0:T(512)(128)(4,1)} %compare_and_fusion.15) | copy-start | bytes 1540 | tf_op jit(solution)/shard_map/while
  123.3 3.4 %copy-start.2 = (f32[8,5,768]{2,0,1:T(8,128)S(1)}, f32[8,5,768]{2,0,1:T(8,128)}, u32[]{:S(2)}) copy-start(f32[8,5,768]{2,0,1:T(8,128)} %copy-done.1) | copy-start | bytes 368644 | tf_op jit(solution)/shard_map/while
  123.3 3.4 %copy-start.6 = (f32[8,10,512]{2,0,1:T(8,128)S(1)}, f32[8,10,512]{2,0,1:T(8,128)}, u32[]{:S(2)}) copy-start(f32[8,10,512]{2,0,1:T(8,128)} %get-tuple-element.260) | copy-start | bytes 491524 | tf_op jit(solution)/shard_map/while
  123.3 3.4 %copy-start.7 = (f32[8,10,512]{2,0,1:T(8,128)S(1)}, f32[8,10,512]{2,0,1:T(8,128)}, u32[]{:S(2)}) copy-start(f32[8,10,512]{2,0,1:T(8,128)} %get-tuple-element.249) | copy-start | bytes 491524 | tf_op jit(solution)/shard_map/while
  123.3 3.4 %copy-start.8 = (f32[8,10,512]{2,0,1:T(8,128)S(1)}, f32[8,10,512]{2,0,1:T(8,128)}, u32[]{:S(2)}) copy-start(f32[8,10,512]{2,0,1:T(8,128)} %get-tuple-element.258) | copy-start | bytes 491524 | tf_op jit(solution)/shard_map/while
  123.3 3.4 %copy-start.9 = (f32[8,10,512]{2,0,1:T(8,128)S(1)}, f32[8,10,512]{2,0,1:T(8,128)}, u32[]{:S(2)}) copy-start(f32[8,10,512]{2,0,1:T(8,128)} %get-tuple-element.247) | copy-start | bytes 491524 | tf_op jit(solution)/shard_map/while
  123.3 3.4 %copy-start.10 = (f32[8,10,512]{2,0,1:T(8,128)S(1)}, f32[8,10,512]{2,0,1:T(8,128)}, u32[]{:S(2)}) copy-start(f32[8,10,512]{2,0,1:T(8,128)} %get-tuple-element.256) | copy-start | bytes 491524 | tf_op jit(solution)/shard_map/while
  123.3 3.4 %copy-start.11 = (f32[8,10,512]{2,0,1:T(8,128)S(1)}, f32[8,10,512]{2,0,1:T(8,128)}, u32[]{:S(2)}) copy-start(f32[8,10,512]{2,0,1:T(8,128)} %get-tuple-element.245) | copy-start | bytes 491524 | tf_op jit(solution)/shard_map/while
  123.3 3.4 %copy-start.12 = (f32[8,10,512]{2,0,1:T(8,128)S(1)}, f32[8,10,512]{2,0,1:T(8,128)}, u32[]{:S(2)}) copy-start(f32[8,10,512]{2,0,1:T(8,128)} %get-tuple-element.254) | copy-start | bytes 491524 | tf_op jit(solution)/shard_map/while
  123.3 3.4 %copy-start.13 = (f32[8,10,512]{2,0,1:T(8,128)S(1)}, f32[8,10,512]{2,0,1:T(8,128)}, u32[]{:S(2)}) copy-start(f32[8,10,512]{2,0,1:T(8,128)} %get-tuple-element.243) | copy-start | bytes 491524 | tf_op jit(solution)/shard_map/while
  123.3 3.4 %copy-start.22 = (f32[1,512]{1,0:T(1,128)S(1)}, f32[1,512]{1,0:T(1,128)}, u32[]{:S(2)}) copy-start(f32[1,512]{1,0:T(1,128)} %get-tuple-element.257) | copy-start | bytes 6148 | tf_op jit(solution)/shard_map/while
  123.4 3.4 %copy-start.23 = (f32[1,512]{1,0:T(1,128)S(1)}, f32[1,512]{1,0:T(1,128)}, u32[]{:S(2)}) copy-start(f32[1,512]{1,0:T(1,128)} %get-tuple-element.259) | copy-start | bytes 6148 | tf_op jit(solution)/shard_map/while
  123.4 3.4 %copy-start.24 = (bf16[2,8,5,512]{3,1,2,0:T(8,128)(2,1)S(1)}, bf16[2,8,5,512]{3,1,2,0:T(8,128)(2,1)}, u32[]{:S(2)}) copy-start(bf16[2,8,5,512]{3,1,2,0:T(8,128)(2,1)} %get-tuple-element.272) | copy-start | bytes 245764 | tf_op jit(solution)/shard_map/while
  189.2 7.4 %copy-start.28 = (pred[512]{0:T(512)(128)(4,1)S(1)}, pred[512]{0:T(512)(128)(4,1)}, u32[]{:S(2)}) copy-start(pred[512]{0:T(512)(128)(4,1)} %compare_and_fusion.17) | copy-start | bytes 1540 | tf_op jit(solution)/shard_map/while
  196.6 7.4 %copy-start.27 = (pred[512]{0:T(512)(128)(4,1)S(1)}, pred[512]{0:T(512)(128)(4,1)}, u32[]{:S(2)}) copy-start(pred[512]{0:T(512)(128)(4,1)} %compare_and_fusion.16) | copy-start | bytes 1540 | tf_op jit(solution)/shard_map/while
  211.3 6.1 %copy-start.18 = (f32[1,512]{1,0:T(1,128)S(1)}, f32[1,512]{1,0:T(1,128)}, u32[]{:S(2)}) copy-start(f32[1,512]{1,0:T(1,128)} %get-tuple-element.261) | copy-start | bytes 6148 | tf_op jit(solution)/shard_map/while
  211.3 6.1 %copy-start.19 = (f32[1,512]{1,0:T(1,128)S(1)}, f32[1,512]{1,0:T(1,128)}, u32[]{:S(2)}) copy-start(f32[1,512]{1,0:T(1,128)} %get-tuple-element.251) | copy-start | bytes 6148 | tf_op jit(solution)/shard_map/while
  211.3 6.1 %copy-start.20 = (f32[1,512]{1,0:T(1,128)S(1)}, f32[1,512]{1,0:T(1,128)}, u32[]{:S(2)}) copy-start(f32[1,512]{1,0:T(1,128)} %get-tuple-element.253) | copy-start | bytes 6148 | tf_op jit(solution)/shard_map/while
  211.3 6.1 %copy-start.21 = (f32[1,512]{1,0:T(1,128)S(1)}, f32[1,512]{1,0:T(1,128)}, u32[]{:S(2)}) copy-start(f32[1,512]{1,0:T(1,128)} %get-tuple-element.255) | copy-start | bytes 6148 | tf_op jit(solution)/shard_map/while
  214.0 3.3 %copy-start.5 = (f32[512,8,10]{0,1,2:T(8,128)S(1)}, f32[512,8,10]{0,1,2:T(8,128)}, u32[]{:S(2)}) copy-start(f32[512,8,10]{0,1,2:T(8,128)} %copy.155) | copy-start | bytes 491524 | tf_op jit(solution)/shard_map/while
  214.0 3.3 %copy-start.26 = (pred[512]{0:T(512)(128)(4,1)S(1)}, pred[512]{0:T(512)(128)(4,1)}, u32[]{:S(2)}) copy-start(pred[512]{0:T(512)(128)(4,1)} %compare_and_fusion.15) | copy-start | bytes 1540 | tf_op jit(solution)/shard_map/while
  214.0 3.4 %copy-start.2 = (f32[8,5,768]{2,0,1:T(8,128)S(1)}, f32[8,5,768]{2,0,1:T(8,128)}, u32[]{:S(2)}) copy-start(f32[8,5,768]{2,0,1:T(8,128)} %copy-done.1) | copy-start | bytes 368644 | tf_op jit(solution)/shard_map/while
  214.0 3.4 %copy-start.6 = (f32[8,10,512]{2,0,1:T(8,128)S(1)}, f32[8,10,512]{2,0,1:T(8,128)}, u32[]{:S(2)}) copy-start(f32[8,10,512]{2,0,1:T(8,128)} %get-tuple-element.260) | copy-start | bytes 491524 | tf_op jit(solution)/shard_map/while
  214.0 3.4 %copy-start.7 = (f32[8,10,512]{2,0,1:T(8,128)S(1)}, f32[8,10,512]{2,0,1:T(8,128)}, u32[]{:S(2)}) copy-start(f32[8,10,512]{2,0,1:T(8,128)} %get-tuple-element.249) | copy-start | bytes 491524 | tf_op jit(solution)/shard_map/while
  214.1 3.4 %copy-start.8 = (f32[8,10,512]{2,0,1:T(8,128)S(1)}, f32[8,10,512]{2,0,1:T(8,128)}, u32[]{:S(2)}) copy-start(f32[8,10,512]{2,0,1:T(8,128)} %get-tuple-element.258) | copy-start | bytes 491524 | tf_op jit(solution)/shard_map/while
  214.1 3.4 %copy-start.9 = (f32[8,10,512]{2,0,1:T(8,128)S(1)}, f32[8,10,512]{2,0,1:T(8,128)}, u32[]{:S(2)}) copy-start(f32[8,10,512]{2,0,1:T(8,128)} %get-tuple-element.247) | copy-start | bytes 491524 | tf_op jit(solution)/shard_map/while
  214.1 3.4 %copy-start.10 = (f32[8,10,512]{2,0,1:T(8,128)S(1)}, f32[8,10,512]{2,0,1:T(8,128)}, u32[]{:S(2)}) copy-start(f32[8,10,512]{2,0,1:T(8,128)} %get-tuple-element.256) | copy-start | bytes 491524 | tf_op jit(solution)/shard_map/while
  214.1 3.4 %copy-start.11 = (f32[8,10,512]{2,0,1:T(8,128)S(1)}, f32[8,10,512]{2,0,1:T(8,128)}, u32[]{:S(2)}) copy-start(f32[8,10,512]{2,0,1:T(8,128)} %get-tuple-element.245) | copy-start | bytes 491524 | tf_op jit(solution)/shard_map/while
  214.1 3.4 %copy-start.12 = (f32[8,10,512]{2,0,1:T(8,128)S(1)}, f32[8,10,512]{2,0,1:T(8,128)}, u32[]{:S(2)}) copy-start(f32[8,10,512]{2,0,1:T(8,128)} %get-tuple-element.254) | copy-start | bytes 491524 | tf_op jit(solution)/shard_map/while
  214.1 3.4 %copy-start.13 = (f32[8,10,512]{2,0,1:T(8,128)S(1)}, f32[8,10,512]{2,0,1:T(8,128)}, u32[]{:S(2)}) copy-start(f32[8,10,512]{2,0,1:T(8,128)} %get-tuple-element.243) | copy-start | bytes 491524 | tf_op jit(solution)/shard_map/while
  214.1 3.4 %copy-start.22 = (f32[1,512]{1,0:T(1,128)S(1)}, f32[1,512]{1,0:T(1,128)}, u32[]{:S(2)}) copy-start(f32[1,512]{1,0:T(1,128)} %get-tuple-element.257) | copy-start | bytes 6148 | tf_op jit(solution)/shard_map/while
  214.1 3.4 %copy-start.23 = (f32[1,512]{1,0:T(1,128)S(1)}, f32[1,512]{1,0:T(1,128)}, u32[]{:S(2)}) copy-start(f32[1,512]{1,0:T(1,128)} %get-tuple-element.259) | copy-start | bytes 6148 | tf_op jit(solution)/shard_map/while
  214.1 3.4 %copy-start.24 = (bf16[2,8,5,512]{3,1,2,0:T(8,128)(2,1)S(1)}, bf16[2,8,5,512]{3,1,2,0:T(8,128)(2,1)}, u32[]{:S(2)}) copy-start(bf16[2,8,5,512]{3,1,2,0:T(8,128)(2,1)} %get-tuple-element.272) | copy-start | bytes 245764 | tf_op jit(solution)/shard_map/while
  (10 other events, 18.2 us)
where the time goes:
time: 232 us; the launch traced here: 230 us
  local copies, waits for them, and re-layouts  154 us (66%)
  other arithmetic  35.5 us (15%)
  blocking collectives  20.3 us (9%)
  starting transfers between devices  10.6 us (5%)
  waiting for transfers between devices  6.83 us (3%)
    gather x48, local copies, waits for them, and re-layouts, face_flux(): taken = jnp.take(stacked, neighbors[face_index], axis=2)  133 us
    select_n x24, other arithmetic, face_flux(): taken = jnp.take(stacked, neighbors[face_index], axis=2)  15.6 us
    psum x1, blocking collectives, local(): return lax.psum(closure_part, 'cell')  10.7 us
    ppermute x4, starting transfers between devices, from_behind(): return lax.ppermute(shard, axis, pairs)  10.6 us
    all_gather x1, blocking collectives, local(): whole_basis = lax.all_gather(basis, ('snap', 'var'), axis=0, tiled=True)  9.68 us
    concatenate x4, local copies, waits for them, and re-layouts, face_flux(): stacked = jnp.concatenate([extended, product], axis=1)  8.67 us
    ppermute x4, waiting for transfers between devices, from_behind(): return lax.ppermute(shard, axis, pairs)  6.83 us
    and x12, other arithmetic, face_flux(): taken = jnp.take(stacked, neighbors[face_index], axis=2)  6.67 us
  transfers between devices with their start and end apart: 4, of which 3 were waited for; matrix products, arithmetic and copies ran while one was open for 1% of the time, Pallas kernels for 0%

commit v1 on v0

--- a/solution.py
+++ b/solution.py
@@ -69,7 +69,7 @@
     closure_part = lax.dot_general(
         weighted_flat, basis_flat, contract, preferred_element_type=jnp.float32
     )
-    return lax.psum(closure_part, "cell")
+    return jnp.sum(lax.all_gather(closure_part, "cell"), axis=0)
 
 
 def solution(mesh):

time: 232 us -> 236 us (1.017)
  blocking collectives: 20.3 us -> 23 us
    all_gather x0 -> x1, blocking collectives: none -> 13.3 us  [local(): return jnp.sum(lax.all_gather(closure_part, 'cell'), axis=0)]
    psum x1 -> x0, blocking collectives: 10.7 us -> none  [local(): return lax.psum(closure_part, 'cell')]
where the time goes in v1:
time: 236 us; the launch traced here: 234 us
  local copies, waits for them, and re-layouts  154 us (65%)
  other arithmetic  36.1 us (15%)
  blocking collectives  23 us (10%)
  starting transfers between devices  10.6 us (4%)
  waiting for transfers between devices  6.83 us (3%)
    gather x48, local copies, waits for them, and re-layouts, face_flux(): taken = jnp.take(stacked, neighbors[face_index], axis=2)  133 us
    select_n x24, other arithmetic, face_flux(): taken = jnp.take(stacked, neighbors[face_index], axis=2)  15.6 us
    all_gather x1, blocking collectives, local(): return jnp.sum(lax.all_gather(closure_part, 'cell'), axis=0)  13.3 us
    ppermute x4, starting transfers between devices, from_behind(): return lax.ppermute(shard, axis, pairs)  10.6 us
    all_gather x1, blocking collectives, local(): whole_basis = lax.all_gather(basis, ('snap', 'var'), axis=0, tiled=True)  9.68 us
    concatenate x4, local copies, waits for them, and re-layouts, face_flux(): stacked = jnp.concatenate([extended, product], axis=1)  8.67 us
    ppermute x4, waiting for transfers between devices, from_behind(): return lax.ppermute(shard, axis, pairs)  6.83 us
    and x12, other arithmetic, face_flux(): taken = jnp.take(stacked, neighbors[face_index], axis=2)  6.67 us
  transfers between devices with their start and end apart: 4, of which 3 were waited for; matrix products, arithmetic and copies ran while one was open for 1% of the time, Pallas kernels for 0%

profile of v1, /device:TPU:0, one launch (start us, length us, event | category | flops | bytes accessed | tf_op | source)
XLA Modules:
  0.0 233.7 jit_solution(14607476594043309886)
XLA Ops:
  0.8 9.7 %all_gather.9 = bf16[128,5,512]{2,0,1:T(8,128)(2,1)S(1)} all-gather(bf16[32,5,512]{2,0,1:T(8,128)(2,1)} %param.16), channel_id=1, replica_groups=mesh['grp'=2,'cell'=4,'snap'=2,'var'=2] {'snap','var'}, dimensions={0}, use_global_device_ids=true | all-gather | bytes 819200 | tf_op jit(solution)/shard_map/all_gather | solution.py:42
  15.2 3.5 %collective-permute-start = (bf16[16,5,128]{0,1,2:T(8,128)(2,1)}, bf16[16,5,128]{0,1,2:T(8,128)(2,1)S(1)}, u32[]{:S(2)}, u32[]{:S(2)}) collective-permute-start(bf16[16,5,128]{0,1,2:T(8,128)(2,1)} %get-tuple-element.158), channel_id=1, source_target_pairs={{0,4},{4,8},{8,12},{1,5},{5,9},{9,13},{2,6},{6,10},{10,14},{3,7},{... | collective-permute-start | bytes 61448 | tf_op jit(solution)/shard_map/ppermute | solution.py:13
  21.6 4.6 %collective-permute-start.2 = (bf16[16,5,128]{0,1,2:T(8,128)(2,1)}, bf16[16,5,128]{0,1,2:T(8,128)(2,1)S(1)}, u32[]{:S(2)}, u32[]{:S(2)}) collective-permute-start(bf16[16,5,128]{0,1,2:T(8,128)(2,1)} %get-tuple-element.157), channel_id=1, source_target_pairs={{0,4},{4,8},{8,12},{1,5},{5,9},{9,13},{2,6},{6,10},{10,14},{3,7},{... | collective-permute-start | bytes 61448 | tf_op jit(solution)/shard_map/ppermute | solution.py:13
  32.1 4.0 %collective-permute-done.3 = bf16[16,5,128]{0,1,2:T(8,128)(2,1)S(1)} collective-permute-done((bf16[16,5,128]{0,1,2:T(8,128)(2,1)S(1)}, bf16[16,5,128]{0,1,2:T(8,128)(2,1)S(1)}, u32[]{:S(2)}, u32[]{:S(2)}) %collective-permute-start.3) | collective-permute-done | bytes 20512 | tf_op jit(solution)/shard_map/ppermute | solution.py:13
  36.9 181.6 %while.11 = (s32[]{:T(128)}, bf16[2,8,5,512]{3,1,2,0:T(8,128)(2,1)}, f32[5,512]{1,0:T(8,128)S(1)}, f32[6,512]{1,0:T(8,128)}, bf16[2,8,5,768]{3,1,0,2:T(8,128)(2,...) while((s32[]{:T(128)}, ...), condition=%wide.region_1.4_spmd.clone, body=%wide.region_0.3_spmd.clone.sunk | while | flops 2576898 | bytes 26133308 | solution.py:66
  49.7 2.8 %gather_fusion.11 = f32[512,8,10]{2,1,0:T(8,128)} fusion(f32[8,10,768]{1,0,2:T(8,128)S(1)} %copy.153, s32[1024]{0:T(1024)} %pad_clamp_fusion.19), kind=kCustom, calls=%fused_computation.10.clone.clone.1 | custom fusion | bytes 329728 | tf_op jit(solution)/shard_map/while/body/eval_jaxpr/jit(_take)/gather | solution.py:25
  52.5 2.9 %copy.164 = f32[512,8,10]{0,1,2:T(8,128)} copy(f32[512,8,10]{2,1,0:T(8,128)} %gather_fusion.11) | data formatting | bytes 327680 | tf_op jit(solution)/shard_map/while/body/eval_jaxpr/jit(_take)/gather | solution.py:25
  55.4 2.7 %gather_fusion.9 = f32[512,8,10]{2,1,0:T(8,128)} fusion(f32[8,10,768]{1,0,2:T(8,128)S(1)} %copy.153, s32[1024]{0:T(1024)S(1)} %pad_clamp_fusion.18), kind=kCustom, calls=%fused_computation.11.clone.clone.1 | custom fusion | bytes 329728 | tf_op jit(solution)/shard_map/while/body/eval_jaxpr/jit(_take)/gather | solution.py:25
  58.1 2.9 %copy.162 = f32[512,8,10]{0,1,2:T(8,128)} copy(f32[512,8,10]{2,1,0:T(8,128)} %gather_fusion.9) | data formatting | bytes 327680 | tf_op jit(solution)/shard_map/while/body/eval_jaxpr/jit(_take)/gather | solution.py:25
  61.0 2.7 %gather_fusion.7 = f32[512,8,10]{2,1,0:T(8,128)} fusion(f32[8,10,768]{1,0,2:T(8,128)S(1)} %copy.153, s32[1024]{0:T(1024)S(1)} %pad_clamp_fusion.17), kind=kCustom, calls=%fused_computation.12.clone.clone.1 | custom fusion | bytes 329728 | tf_op jit(solution)/shard_map/while/body/eval_jaxpr/jit(_take)/gather | solution.py:25
  63.6 2.9 %copy.160 = f32[512,8,10]{0,1,2:T(8,128)} copy(f32[512,8,10]{2,1,0:T(8,128)} %gather_fusion.7) | data formatting | bytes 327680 | tf_op jit(solution)/shard_map/while/body/eval_jaxpr/jit(_take)/gather | solution.py:25
  66.5 2.7 %gather_fusion.5 = f32[512,8,10]{2,1,0:T(8,128)} fusion(f32[8,10,768]{1,0,2:T(8,128)S(1)} %copy.153, s32[1024]{0:T(1024)S(1)} %pad_clamp_fusion.16), kind=kCustom, calls=%fused_computation.13.clone.clone.1 | custom fusion | bytes 329728 | tf_op jit(solution)/shard_map/while/body/eval_jaxpr/jit(_take)/gather | solution.py:25
  69.2 2.9 %copy.158 = f32[512,8,10]{0,1,2:T(8,128)} copy(f32[512,8,10]{2,1,0:T(8,128)} %gather_fusion.5) | data formatting | bytes 327680 | tf_op jit(solution)/shard_map/while/body/eval_jaxpr/jit(_take)/gather | solution.py:25
  72.1 2.7 %gather_fusion.3 = f32[512,8,10]{2,1,0:T(8,128)} fusion(f32[8,10,768]{1,0,2:T(8,128)S(1)} %copy.153, s32[1024]{0:T(1024)S(1)} %pad_clamp_fusion.15), kind=kCustom, calls=%fused_computation.14.clone.clone.1 | custom fusion | bytes 329728 | tf_op jit(solution)/shard_map/while/body/eval_jaxpr/jit(_take)/gather | solution.py:25
  74.8 2.9 %copy.156 = f32[512,8,10]{0,1,2:T(8,128)} copy(f32[512,8,10]{2,1,0:T(8,128)} %gather_fusion.3) | data formatting | bytes 327680 | tf_op jit(solution)/shard_map/while/body/eval_jaxpr/jit(_take)/gather | solution.py:25
  77.7 2.7 %gather_fusion.1 = f32[512,8,10]{2,1,0:T(8,128)} fusion(f32[8,10,768]{1,0,2:T(8,128)S(1)} %copy.153, s32[1024]{0:T(1024)S(1)} %pad_clamp_fusion.14), kind=kCustom, calls=%fused_computation.15.clone.clone.1 | custom fusion | bytes 329728 | tf_op jit(solution)/shard_map/while/body/eval_jaxpr/jit(_take)/gather | solution.py:25
  80.3 2.9 %copy.154 = f32[512,8,10]{0,1,2:T(8,128)} copy(f32[512,8,10]{2,1,0:T(8,128)} %gather_fusion.1) | data formatting | bytes 327680 | tf_op jit(solution)/shard_map/while/body/eval_jaxpr/jit(_take)/gather | solution.py:25
  85.4 2.8 %gather_fusion.10 = f32[512,8,10]{2,1,0:T(8,128)} fusion(f32[8,10,768]{1,0,2:T(8,128)S(1)} %copy.151, s32[1024]{0:T(1024)} %pad_clamp_fusion.19), kind=kCustom, calls=%fused_computation.1.clone.clone.1 | custom fusion | bytes 329728 | tf_op jit(solution)/shard_map/while/body/eval_jaxpr/jit(_take)/gather | solution.py:25
  88.2 2.9 %copy.163 = f32[512,8,10]{0,1,2:T(8,128)} copy(f32[512,8,10]{2,1,0:T(8,128)} %gather_fusion.10) | data formatting | bytes 327680 | tf_op jit(solution)/shard_map/while/body/eval_jaxpr/jit(_take)/gather | solution.py:25
  95.5 2.9 %copy.161 = f32[512,8,10]{0,1,2:T(8,128)} copy(f32[512,8,10]{2,1,0:T(8,128)} %gather_fusion.8) | data formatting | bytes 327680 | tf_op jit(solution)/shard_map/while/body/eval_jaxpr/jit(_take)/gather | solution.py:25
  100.2 2.7 %gather_fusion.6 = f32[512,8,10]{2,1,0:T(8,128)} fusion(f32[8,10,768]{1,0,2:T(8,128)S(1)} %copy.151, s32[1024]{0:T(1024)S(1)} %pad_clamp_fusion.17), kind=kCustom, calls=%fused_computation.6.clone.clone.1 | custom fusion | bytes 329728 | tf_op jit(solution)/shard_map/while/body/eval_jaxpr/jit(_take)/gather | solution.py:25
  102.9 2.9 %copy.159 = f32[512,8,10]{0,1,2:T(8,128)} copy(f32[512,8,10]{2,1,0:T(8,128)} %gather_fusion.6) | data formatting | bytes 327680 | tf_op jit(solution)/shard_map/while/body/eval_jaxpr/jit(_take)/gather | solution.py:25
  107.6 2.7 %gather_fusion.4 = f32[512,8,10]{2,1,0:T(8,128)} fusion(f32[8,10,768]{1,0,2:T(8,128)S(1)} %copy.151, s32[1024]{0:T(1024)S(1)} %pad_clamp_fusion.16), kind=kCustom, calls=%fused_computation.7.clone.clone.1 | custom fusion | bytes 329728 | tf_op jit(solution)/shard_map/while/body/eval_jaxpr/jit(_take)/gather | solution.py:25
  110.3 2.9 %copy.157 = f32[512,8,10]{0,1,2:T(8,128)} copy(f32[512,8,10]{2,1,0:T(8,128)} %gather_fusion.4) | data formatting | bytes 327680 | tf_op jit(solution)/shard_map/while/body/eval_jaxpr/jit(_take)/gather | solution.py:25
  114.9 2.7 %gather_fusion.2 = f32[512,8,10]{2,1,0:T(8,128)} fusion(f32[8,10,768]{1,0,2:T(8,128)S(1)} %copy.151, s32[1024]{0:T(1024)S(1)} %pad_clamp_fusion.15), kind=kCustom, calls=%fused_computation.8.clone.clone.1 | custom fusion | bytes 329728 | tf_op jit(solution)/shard_map/while/body/eval_jaxpr/jit(_take)/gather | solution.py:25
  117.6 2.9 %copy.155 = f32[512,8,10]{0,1,2:T(8,128)} copy(f32[512,8,10]{2,1,0:T(8,128)} %gather_fusion.2) | data formatting | bytes 327680 | tf_op jit(solution)/shard_map/while/body/eval_jaxpr/jit(_take)/gather | solution.py:25
  120.5 2.7 %gather_fusion = f32[512,8,10]{2,1,0:T(8,128)} fusion(f32[8,10,768]{1,0,2:T(8,128)S(1)} %copy.151, s32[1024]{0:T(1024)S(1)} %pad_clamp_fusion.14), kind=kCustom, calls=%fused_computation.9.clone.clone.1 | custom fusion | bytes 329728 | tf_op jit(solution)/shard_map/while/body/eval_jaxpr/jit(_take)/gather | solution.py:25
  140.5 2.8 %gather_fusion.11 = f32[512,8,10]{2,1,0:T(8,128)} fusion(f32[8,10,768]{1,0,2:T(8,128)S(1)} %copy.153, s32[1024]{0:T(1024)} %pad_clamp_fusion.19), kind=kCustom, calls=%fused_computation.10.clone.clone.1 | custom fusion | bytes 329728 | tf_op jit(solution)/shard_map/while/body/eval_jaxpr/jit(_take)/gather | solution.py:25
  143.3 2.9 %copy.164 = f32[512,8,10]{0,1,2:T(8,128)} copy(f32[512,8,10]{2,1,0:T(8,128)} %gather_fusion.11) | data formatting | bytes 327680 | tf_op jit(solution)/shard_map/while/body/eval_jaxpr/jit(_take)/gather | solution.py:25
  146.2 2.7 %gather_fusion.9 = f32[512,8,10]{2,1,0:T(8,128)} fusion(f32[8,10,768]{1,0,2:T(8,128)S(1)} %copy.153, s32[1024]{0:T(1024)S(1)} %pad_clamp_fusion.18), kind=kCustom, calls=%fused_computation.11.clone.clone.1 | custom fusion | bytes 329728 | tf_op jit(solution)/shard_map/while/body/eval_jaxpr/jit(_take)/gather | solution.py:25
  148.9 2.9 %copy.162 = f32[512,8,10]{0,1,2:T(8,128)} copy(f32[512,8,10]{2,1,0:T(8,128)} %gather_fusion.9) | data formatting | bytes 327680 | tf_op jit(solution)/shard_map/while/body/eval_jaxpr/jit(_take)/gather | solution.py:25
  151.7 2.7 %gather_fusion.7 = f32[512,8,10]{2,1,0:T(8,128)} fusion(f32[8,10,768]{1,0,2:T(8,128)S(1)} %copy.153, s32[1024]{0:T(1024)S(1)} %pad_clamp_fusion.17), kind=kCustom, calls=%fused_computation.12.clone.clone.1 | custom fusion | bytes 329728 | tf_op jit(solution)/shard_map/while/body/eval_jaxpr/jit(_take)/gather | solution.py:25
  154.4 2.9 %copy.160 = f32[512,8,10]{0,1,2:T(8,128)} copy(f32[512,8,10]{2,1,0:T(8,128)} %gather_fusion.7) | data formatting | bytes 327680 | tf_op jit(solution)/shard_map/while/body/eval_jaxpr/jit(_take)/gather | solution.py:25
  157.3 2.7 %gather_fusion.5 = f32[512,8,10]{2,1,0:T(8,128)} fusion(f32[8,10,768]{1,0,2:T(8,128)S(1)} %copy.153, s32[1024]{0:T(1024)S(1)} %pad_clamp_fusion.16), kind=kCustom, calls=%fused_computation.13.clone.clone.1 | custom fusion | bytes 329728 | tf_op jit(solution)/shard_map/while/body/eval_jaxpr/jit(_take)/gather | solution.py:25
  160.0 2.9 %copy.158 = f32[512,8,10]{0,1,2:T(8,128)} copy(f32[512,8,10]{2,1,0:T(8,128)} %gather_fusion.5) | data formatting | bytes 327680 | tf_op jit(solution)/shard_map/while/body/eval_jaxpr/jit(_take)/gather | solution.py:25
  165.6 2.9 %copy.156 = f32[512,8,10]{0,1,2:T(8,128)} copy(f32[512,8,10]{2,1,0:T(8,128)} %gather_fusion.3) | data formatting | bytes 327680 | tf_op jit(solution)/shard_map/while/body/eval_jaxpr/jit(_take)/gather | solution.py:25
  171.1 2.9 %copy.154 = f32[512,8,10]{0,1,2:T(8,128)} copy(f32[512,8,10]{2,1,0:T(8,128)} %gather_fusion.1) | data formatting | bytes 327680 | tf_op jit(solution)/shard_map/while/body/eval_jaxpr/jit(_take)/gather | solution.py:25
  176.2 2.8 %gather_fusion.10 = f32[512,8,10]{2,1,0:T(8,128)} fusion(f32[8,10,768]{1,0,2:T(8,128)S(1)} %copy.151, s32[1024]{0:T(1024)} %pad_clamp_fusion.19), kind=kCustom, calls=%fused_computation.1.clone.clone.1 | custom fusion | bytes 329728 | tf_op jit(solution)/shard_map/while/body/eval_jaxpr/jit(_take)/gather | solution.py:25
  179.0 2.9 %copy.163 = f32[512,8,10]{0,1,2:T(8,128)} copy(f32[512,8,10]{2,1,0:T(8,128)} %gather_fusion.10) | data formatting | bytes 327680 | tf_op jit(solution)/shard_map/while/body/eval_jaxpr/jit(_take)/gather | solution.py:25
  186.3 2.9 %copy.161 = f32[512,8,10]{0,1,2:T(8,128)} copy(f32[512,8,10]{2,1,0:T(8,128)} %gather_fusion.8) | data formatting | bytes 327680 | tf_op jit(solution)/shard_map/while/body/eval_jaxpr/jit(_take)/gather | solution.py:25
  191.0 2.7 %gather_fusion.6 = f32[512,8,10]{2,1,0:T(8,128)} fusion(f32[8,10,768]{1,0,2:T(8,128)S(1)} %copy.151, s32[1024]{0:T(1024)S(1)} %pad_clamp_fusion.17), kind=kCustom, calls=%fused_computation.6.clone.clone.1 | custom fusion | bytes 329728 | tf_op jit(solution)/shard_map/while/body/eval_jaxpr/jit(_take)/gather | solution.py:25
  193.7 2.9 %copy.159 = f32[512,8,10]{0,1,2:T(8,128)} copy(f32[512,8,10]{2,1,0:T(8,128)} %gather_fusion.6) | data formatting | bytes 327680 | tf_op jit(solution)/shard_map/while/body/eval_jaxpr/jit(_take)/gather | solution.py:25
  198.3 2.7 %gather_fusion.4 = f32[512,8,10]{2,1,0:T(8,128)} fusion(f32[8,10,768]{1,0,2:T(8,128)S(1)} %copy.151, s32[1024]{0:T(1024)S(1)} %pad_clamp_fusion.16), kind=kCustom, calls=%fused_computation.7.clone.clone.1 | custom fusion | bytes 329728 | tf_op jit(solution)/shard_map/while/body/eval_jaxpr/jit(_take)/gather | solution.py:25
  201.1 2.9 %copy.157 = f32[512,8,10]{0,1,2:T(8,128)} copy(f32[512,8,10]{2,1,0:T(8,128)} %gather_fusion.4) | data formatting | bytes 327680 | tf_op jit(solution)/shard_map/while/body/eval_jaxpr/jit(_take)/gather | solution.py:25
  205.7 2.7 %gather_fusion.2 = f32[512,8,10]{2,1,0:T(8,128)} fusion(f32[8,10,768]{1,0,2:T(8,128)S(1)} %copy.151, s32[1024]{0:T(1024)S(1)} %pad_clamp_fusion.15), kind=kCustom, calls=%fused_computation.8.clone.clone.1 | custom fusion | bytes 329728 | tf_op jit(solution)/shard_map/while/body/eval_jaxpr/jit(_take)/gather | solution.py:25
  208.4 2.9 %copy.155 = f32[512,8,10]{0,1,2:T(8,128)} copy(f32[512,8,10]{2,1,0:T(8,128)} %gather_fusion.2) | data formatting | bytes 327680 | tf_op jit(solution)/shard_map/while/body/eval_jaxpr/jit(_take)/gather | solution.py:25
  211.3 2.7 %gather_fusion = f32[512,8,10]{2,1,0:T(8,128)} fusion(f32[8,10,768]{1,0,2:T(8,128)S(1)} %copy.151, s32[1024]{0:T(1024)S(1)} %pad_clamp_fusion.14), kind=kCustom, calls=%fused_computation.9.clone.clone.1 | custom fusion | bytes 329728 | tf_op jit(solution)/shard_map/while/body/eval_jaxpr/jit(_take)/gather | solution.py:25
  219.8 13.3 %all-gather = f32[64,128]{1,0:T(8,128)S(1)} all-gather(f32[16,128]{1,0:T(8,128)S(1)} %fusion.66), channel_id=2, replica_groups=mesh['grp'=2,'cell'=4,'snap'=2,'var'=2] {'cell'}, dimensions={0}, use_global_device_ids=true | all-gather | bytes 40960 | tf_op jit(solution)/shard_map/all_gather | solution.py:72
  (218 shorter events, 79.3 us)
Async XLA Ops:
  0.0 10.8 %copy-start = (bf16[16,128]{1,0:T(8,128)(2,1)S(1)}, bf16[16,128]{1,0:T(8,128)(2,1)}, u32[]{:S(2)}) copy-start(bf16[16,128]{1,0:T(8,128)(2,1)} %param.15) | copy-start | bytes 12292
  0.8 11.3 %copy-start.17 = (bf16[16,5,512]{2,0,1:T(8,128)(2,1)S(1)}, bf16[16,5,512]{2,0,1:T(8,128)(2,1)}, u32[]{:S(2)}) copy-start(bf16[16,5,512]{2,0,1:T(8,128)(2,1)} %param.14) | copy-start | bytes 245764
  10.8 4.4 %copy-start.14 = (bf16[128,5,512]{0,2,1:T(8,128)(2,1)}, bf16[128,5,512]{0,2,1:T(8,128)(2,1)S(1)}, u32[]{:S(2)}) copy-start(bf16[128,5,512]{0,2,1:T(8,128)(2,1)S(1)} %copy.124) | copy-start | bytes 1966084
  12.8 24.1 %copy-start.15 = (f32[5,512]{1,0:T(8,128)S(1)}, f32[5,512]{1,0:T(8,128)}, u32[]{:S(2)}) copy-start(f32[5,512]{1,0:T(8,128)} %param.17) | copy-start | bytes 30724
  15.2 12.9 %collective-permute-start = (bf16[16,5,128]{0,1,2:T(8,128)(2,1)}, bf16[16,5,128]{0,1,2:T(8,128)(2,1)S(1)}, u32[]{:S(2)}, u32[]{:S(2)}) collective-permute-start(bf16[16,5,128]{0,1,2:T(8,128)(2,1)} %get-tuple-element.158), channel_id=1, source_target_pairs={{0,4},{4,8},{8,12},{1,5},{5,9},{9,13},{2,6},{6,10},{10,14},{3,7},{... | collective-permute-start | bytes 61448 | tf_op jit(solution)/shard_map/ppermute | solution.py:13
  20.3 10.4 %collective-permute-start.1 = (bf16[16,5,128]{0,1,2:T(8,128)(2,1)S(1)}, bf16[16,5,128]{0,1,2:T(8,128)(2,1)S(1)}, u32[]{:S(2)}, u32[]{:S(2)}) collective-permute-start(bf16[16,5,128]{0,1,2:T(8,128)(2,1)S(1)} %get-tuple-element.160), channel_id=1, source_target_pairs={{4,0},{8,4},{12,8},{5,1},{9,5},{13,9},{6,2},{10,6},{14,10},{7,3},{... | collective-permute-start | bytes 61448 | tf_op jit(solution)/shard_map/ppermute | solution.py:13
  21.6 10.4 %collective-permute-start.2 = (bf16[16,5,128]{0,1,2:T(8,128)(2,1)}, bf16[16,5,128]{0,1,2:T(8,128)(2,1)S(1)}, u32[]{:S(2)}, u32[]{:S(2)}) collective-permute-start(bf16[16,5,128]{0,1,2:T(8,128)(2,1)} %get-tuple-element.157), channel_id=1, source_target_pairs={{0,4},{4,8},{8,12},{1,5},{5,9},{9,13},{2,6},{6,10},{10,14},{3,7},{... | collective-permute-start | bytes 61448 | tf_op jit(solution)/shard_map/ppermute | solution.py:13
  26.2 9.9 %collective-permute-start.3 = (bf16[16,5,128]{0,1,2:T(8,128)(2,1)S(1)}, bf16[16,5,128]{0,1,2:T(8,128)(2,1)S(1)}, u32[]{:S(2)}, u32[]{:S(2)}) collective-permute-start(bf16[16,5,128]{0,1,2:T(8,128)(2,1)S(1)} %get-tuple-element.159), channel_id=1, source_target_pairs={{4,0},{8,4},{12,8},{5,1},{9,5},{13,9},{6,2},{10,6},{14,10},{7,3},{... | collective-permute-start | bytes 61448 | tf_op jit(solution)/shard_map/ppermute | solution.py:13
  98.4 7.4 %copy-start.28 = (pred[512]{0:T(512)(128)(4,1)S(1)}, pred[512]{0:T(512)(128)(4,1)}, u32[]{:S(2)}) copy-start(pred[512]{0:T(512)(128)(4,1)} %compare_and_fusion.17) | copy-start | bytes 1540 | tf_op jit(solution)/shard_map/while
  105.8 7.4 %copy-start.27 = (pred[512]{0:T(512)(128)(4,1)S(1)}, pred[512]{0:T(512)(128)(4,1)}, u32[]{:S(2)}) copy-start(pred[512]{0:T(512)(128)(4,1)} %compare_and_fusion.16) | copy-start | bytes 1540 | tf_op jit(solution)/shard_map/while
  120.5 6.1 %copy-start.18 = (f32[1,512]{1,0:T(1,128)S(1)}, f32[1,512]{1,0:T(1,128)}, u32[]{:S(2)}) copy-start(f32[1,512]{1,0:T(1,128)} %get-tuple-element.261) | copy-start | bytes 6148 | tf_op jit(solution)/shard_map/while
  120.5 6.1 %copy-start.19 = (f32[1,512]{1,0:T(1,128)S(1)}, f32[1,512]{1,0:T(1,128)}, u32[]{:S(2)}) copy-start(f32[1,512]{1,0:T(1,128)} %get-tuple-element.251) | copy-start | bytes 6148 | tf_op jit(solution)/shard_map/while
  120.5 6.1 %copy-start.20 = (f32[1,512]{1,0:T(1,128)S(1)}, f32[1,512]{1,0:T(1,128)}, u32[]{:S(2)}) copy-start(f32[1,512]{1,0:T(1,128)} %get-tuple-element.253) | copy-start | bytes 6148 | tf_op jit(solution)/shard_map/while
  120.5 6.1 %copy-start.21 = (f32[1,512]{1,0:T(1,128)S(1)}, f32[1,512]{1,0:T(1,128)}, u32[]{:S(2)}) copy-start(f32[1,512]{1,0:T(1,128)} %get-tuple-element.255) | copy-start | bytes 6148 | tf_op jit(solution)/shard_map/while
  123.2 3.3 %copy-start.5 = (f32[512,8,10]{0,1,2:T(8,128)S(1)}, f32[512,8,10]{0,1,2:T(8,128)}, u32[]{:S(2)}) copy-start(f32[512,8,10]{0,1,2:T(8,128)} %copy.155) | copy-start | bytes 491524 | tf_op jit(solution)/shard_map/while
  123.2 3.3 %copy-start.26 = (pred[512]{0:T(512)(128)(4,1)S(1)}, pred[512]{0:T(512)(128)(4,1)}, u32[]{:S(2)}) copy-start(pred[512]{0:T(512)(128)(4,1)} %compare_and_fusion.15) | copy-start | bytes 1540 | tf_op jit(solution)/shard_map/while
  123.3 3.4 %copy-start.2 = (f32[8,5,768]{2,0,1:T(8,128)S(1)}, f32[8,5,768]{2,0,1:T(8,128)}, u32[]{:S(2)}) copy-start(f32[8,5,768]{2,0,1:T(8,128)} %copy-done.1) | copy-start | bytes 368644 | tf_op jit(solution)/shard_map/while
  123.3 3.4 %copy-start.6 = (f32[8,10,512]{2,0,1:T(8,128)S(1)}, f32[8,10,512]{2,0,1:T(8,128)}, u32[]{:S(2)}) copy-start(f32[8,10,512]{2,0,1:T(8,128)} %get-tuple-element.260) | copy-start | bytes 491524 | tf_op jit(solution)/shard_map/while
  123.3 3.4 %copy-start.7 = (f32[8,10,512]{2,0,1:T(8,128)S(1)}, f32[8,10,512]{2,0,1:T(8,128)}, u32[]{:S(2)}) copy-start(f32[8,10,512]{2,0,1:T(8,128)} %get-tuple-element.249) | copy-start | bytes 491524 | tf_op jit(solution)/shard_map/while
  123.3 3.4 %copy-start.8 = (f32[8,10,512]{2,0,1:T(8,128)S(1)}, f32[8,10,512]{2,0,1:T(8,128)}, u32[]{:S(2)}) copy-start(f32[8,10,512]{2,0,1:T(8,128)} %get-tuple-element.258) | copy-start | bytes 491524 | tf_op jit(solution)/shard_map/while
  123.3 3.4 %copy-start.9 = (f32[8,10,512]{2,0,1:T(8,128)S(1)}, f32[8,10,512]{2,0,1:T(8,128)}, u32[]{:S(2)}) copy-start(f32[8,10,512]{2,0,1:T(8,128)} %get-tuple-element.247) | copy-start | bytes 491524 | tf_op jit(solution)/shard_map/while
  123.3 3.4 %copy-start.10 = (f32[8,10,512]{2,0,1:T(8,128)S(1)}, f32[8,10,512]{2,0,1:T(8,128)}, u32[]{:S(2)}) copy-start(f32[8,10,512]{2,0,1:T(8,128)} %get-tuple-element.256) | copy-start | bytes 491524 | tf_op jit(solution)/shard_map/while
  123.3 3.4 %copy-start.11 = (f32[8,10,512]{2,0,1:T(8,128)S(1)}, f32[8,10,512]{2,0,1:T(8,128)}, u32[]{:S(2)}) copy-start(f32[8,10,512]{2,0,1:T(8,128)} %get-tuple-element.245) | copy-start | bytes 491524 | tf_op jit(solution)/shard_map/while
  123.3 3.4 %copy-start.12 = (f32[8,10,512]{2,0,1:T(8,128)S(1)}, f32[8,10,512]{2,0,1:T(8,128)}, u32[]{:S(2)}) copy-start(f32[8,10,512]{2,0,1:T(8,128)} %get-tuple-element.254) | copy-start | bytes 491524 | tf_op jit(solution)/shard_map/while
  123.3 3.4 %copy-start.13 = (f32[8,10,512]{2,0,1:T(8,128)S(1)}, f32[8,10,512]{2,0,1:T(8,128)}, u32[]{:S(2)}) copy-start(f32[8,10,512]{2,0,1:T(8,128)} %get-tuple-element.243) | copy-start | bytes 491524 | tf_op jit(solution)/shard_map/while
  123.3 3.4 %copy-start.22 = (f32[1,512]{1,0:T(1,128)S(1)}, f32[1,512]{1,0:T(1,128)}, u32[]{:S(2)}) copy-start(f32[1,512]{1,0:T(1,128)} %get-tuple-element.257) | copy-start | bytes 6148 | tf_op jit(solution)/shard_map/while
  123.4 3.4 %copy-start.23 = (f32[1,512]{1,0:T(1,128)S(1)}, f32[1,512]{1,0:T(1,128)}, u32[]{:S(2)}) copy-start(f32[1,512]{1,0:T(1,128)} %get-tuple-element.259) | copy-start | bytes 6148 | tf_op jit(solution)/shard_map/while
  123.4 3.4 %copy-start.24 = (bf16[2,8,5,512]{3,1,2,0:T(8,128)(2,1)S(1)}, bf16[2,8,5,512]{3,1,2,0:T(8,128)(2,1)}, u32[]{:S(2)}) copy-start(bf16[2,8,5,512]{3,1,2,0:T(8,128)(2,1)} %get-tuple-element.272) | copy-start | bytes 245764 | tf_op jit(solution)/shard_map/while
  189.2 7.4 %copy-start.28 = (pred[512]{0:T(512)(128)(4,1)S(1)}, pred[512]{0:T(512)(128)(4,1)}, u32[]{:S(2)}) copy-start(pred[512]{0:T(512)(128)(4,1)} %compare_and_fusion.17) | copy-start | bytes 1540 | tf_op jit(solution)/shard_map/while
  196.6 7.4 %copy-start.27 = (pred[512]{0:T(512)(128)(4,1)S(1)}, pred[512]{0:T(512)(128)(4,1)}, u32[]{:S(2)}) copy-start(pred[512]{0:T(512)(128)(4,1)} %compare_and_fusion.16) | copy-start | bytes 1540 | tf_op jit(solution)/shard_map/while
  211.3 6.1 %copy-start.18 = (f32[1,512]{1,0:T(1,128)S(1)}, f32[1,512]{1,0:T(1,128)}, u32[]{:S(2)}) copy-start(f32[1,512]{1,0:T(1,128)} %get-tuple-element.261) | copy-start | bytes 6148 | tf_op jit(solution)/shard_map/while
  211.3 6.1 %copy-start.19 = (f32[1,512]{1,0:T(1,128)S(1)}, f32[1,512]{1,0:T(1,128)}, u32[]{:S(2)}) copy-start(f32[1,512]{1,0:T(1,128)} %get-tuple-element.251) | copy-start | bytes 6148 | tf_op jit(solution)/shard_map/while
  211.3 6.1 %copy-start.20 = (f32[1,512]{1,0:T(1,128)S(1)}, f32[1,512]{1,0:T(1,128)}, u32[]{:S(2)}) copy-start(f32[1,512]{1,0:T(1,128)} %get-tuple-element.253) | copy-start | bytes 6148 | tf_op jit(solution)/shard_map/while
  211.3 6.1 %copy-start.21 = (f32[1,512]{1,0:T(1,128)S(1)}, f32[1,512]{1,0:T(1,128)}, u32[]{:S(2)}) copy-start(f32[1,512]{1,0:T(1,128)} %get-tuple-element.255) | copy-start | bytes 6148 | tf_op jit(solution)/shard_map/while
  214.0 3.3 %copy-start.5 = (f32[512,8,10]{0,1,2:T(8,128)S(1)}, f32[512,8,10]{0,1,2:T(8,128)}, u32[]{:S(2)}) copy-start(f32[512,8,10]{0,1,2:T(8,128)} %copy.155) | copy-start | bytes 491524 | tf_op jit(solution)/shard_map/while
  214.0 3.3 %copy-start.26 = (pred[512]{0:T(512)(128)(4,1)S(1)}, pred[512]{0:T(512)(128)(4,1)}, u32[]{:S(2)}) copy-start(pred[512]{0:T(512)(128)(4,1)} %compare_and_fusion.15) | copy-start | bytes 1540 | tf_op jit(solution)/shard_map/while
  214.0 3.4 %copy-start.2 = (f32[8,5,768]{2,0,1:T(8,128)S(1)}, f32[8,5,768]{2,0,1:T(8,128)}, u32[]{:S(2)}) copy-start(f32[8,5,768]{2,0,1:T(8,128)} %copy-done.1) | copy-start | bytes 368644 | tf_op jit(solution)/shard_map/while
  214.0 3.4 %copy-start.6 = (f32[8,10,512]{2,0,1:T(8,128)S(1)}, f32[8,10,512]{2,0,1:T(8,128)}, u32[]{:S(2)}) copy-start(f32[8,10,512]{2,0,1:T(8,128)} %get-tuple-element.260) | copy-start | bytes 491524 | tf_op jit(solution)/shard_map/while
  214.0 3.4 %copy-start.7 = (f32[8,10,512]{2,0,1:T(8,128)S(1)}, f32[8,10,512]{2,0,1:T(8,128)}, u32[]{:S(2)}) copy-start(f32[8,10,512]{2,0,1:T(8,128)} %get-tuple-element.249) | copy-start | bytes 491524 | tf_op jit(solution)/shard_map/while
  214.1 3.4 %copy-start.8 = (f32[8,10,512]{2,0,1:T(8,128)S(1)}, f32[8,10,512]{2,0,1:T(8,128)}, u32[]{:S(2)}) copy-start(f32[8,10,512]{2,0,1:T(8,128)} %get-tuple-element.258) | copy-start | bytes 491524 | tf_op jit(solution)/shard_map/while
  214.1 3.4 %copy-start.9 = (f32[8,10,512]{2,0,1:T(8,128)S(1)}, f32[8,10,512]{2,0,1:T(8,128)}, u32[]{:S(2)}) copy-start(f32[8,10,512]{2,0,1:T(8,128)} %get-tuple-element.247) | copy-start | bytes 491524 | tf_op jit(solution)/shard_map/while
  214.1 3.4 %copy-start.10 = (f32[8,10,512]{2,0,1:T(8,128)S(1)}, f32[8,10,512]{2,0,1:T(8,128)}, u32[]{:S(2)}) copy-start(f32[8,10,512]{2,0,1:T(8,128)} %get-tuple-element.256) | copy-start | bytes 491524 | tf_op jit(solution)/shard_map/while
  214.1 3.4 %copy-start.11 = (f32[8,10,512]{2,0,1:T(8,128)S(1)}, f32[8,10,512]{2,0,1:T(8,128)}, u32[]{:S(2)}) copy-start(f32[8,10,512]{2,0,1:T(8,128)} %get-tuple-element.245) | copy-start | bytes 491524 | tf_op jit(solution)/shard_map/while
  214.1 3.4 %copy-start.12 = (f32[8,10,512]{2,0,1:T(8,128)S(1)}, f32[8,10,512]{2,0,1:T(8,128)}, u32[]{:S(2)}) copy-start(f32[8,10,512]{2,0,1:T(8,128)} %get-tuple-element.254) | copy-start | bytes 491524 | tf_op jit(solution)/shard_map/while
  214.1 3.4 %copy-start.13 = (f32[8,10,512]{2,0,1:T(8,128)S(1)}, f32[8,10,512]{2,0,1:T(8,128)}, u32[]{:S(2)}) copy-start(f32[8,10,512]{2,0,1:T(8,128)} %get-tuple-element.243) | copy-start | bytes 491524 | tf_op jit(solution)/shard_map/while
  214.1 3.4 %copy-start.22 = (f32[1,512]{1,0:T(1,128)S(1)}, f32[1,512]{1,0:T(1,128)}, u32[]{:S(2)}) copy-start(f32[1,512]{1,0:T(1,128)} %get-tuple-element.257) | copy-start | bytes 6148 | tf_op jit(solution)/shard_map/while
  214.1 3.4 %copy-start.23 = (f32[1,512]{1,0:T(1,128)S(1)}, f32[1,512]{1,0:T(1,128)}, u32[]{:S(2)}) copy-start(f32[1,512]{1,0:T(1,128)} %get-tuple-element.259) | copy-start | bytes 6148 | tf_op jit(solution)/shard_map/while
  214.1 3.4 %copy-start.24 = (bf16[2,8,5,512]{3,1,2,0:T(8,128)(2,1)S(1)}, bf16[2,8,5,512]{3,1,2,0:T(8,128)(2,1)}, u32[]{:S(2)}) copy-start(bf16[2,8,5,512]{3,1,2,0:T(8,128)(2,1)} %get-tuple-element.272) | copy-start | bytes 245764 | tf_op jit(solution)/shard_map/while
  (10 other events, 18.2 us)
